TPU v7x, 512 devices: a whole 4x8x8 slice. The times are simulated.
512 devices in a mesh: tp: 8 (over y), vocab: 64 (over x, z, core).
Axes of the slice: x: 4, y: 8, z: 8, core: 2. Of those that a mesh axis runs over, the one named last changes fastest.
Arguments:
- partials: float32 [8, 1024, 8192], P('tp', 'vocab'), may hold values from -2.5 to 2.5
- residual: bfloat16 [1024, 8192], P('vocab', 'tp'), may hold values from -16 to 16
- norm_gain: float32 [8192], P('tp'), may hold values from 0.5 to 1.5
- head_weight: bfloat16 [8192, 98304], P('tp', 'vocab'), may hold values from -8 to 8
- owners: int32 [1024], P('tp'), may hold values from 0 to 63, as said below
- allowed: int32 [1024, 256], P('tp'), may hold values from 0 to 768, as said below
- counts: int32 [1024], P('tp'), may hold values from 1 to 256, as said below
Outputs:
- allowed_logprobs: float32 [2048, 256, 128], P(('tp', 'vocab'))
Inputs may be any that keep to these rules, and one draw needn't show every extreme that they name: `owners`: within each group of 128 consecutive rows no owner has more than 4 rows, and one owner has exactly 4. `allowed`: block b holds vocabulary ids 128 * b to 128 * b + 127. The first counts[r] entries of a row are distinct and ascending, the rest equal 768; at most 4 of a row's blocks lie among blocks 12 * v to 12 * v + 11 for any v, and in each group of rows the rows of one owner reach 4 for every v. `counts`: each group of 128 consecutive rows has a row with 256.
All inputs are finite; a program needn't handle non-finite values.
Results may differ from a plain program's by a relative error of at most 0.00032.
Values sent between devices are 32-bit elements; how exact they have to be, the bound alone decides.
A program may use at most 64 MiB of HBM per device.

v0:
```python
import jax
import jax.numpy as jnp
from jax import lax
from jax.sharding import PartitionSpec as P

EPSILON = 1e-05
BLOCK = 128
KMAX = 4


def slot_ranks(owners):
    row_order = jnp.arange(owners.shape[0], dtype=jnp.int32)
    same_owner = (owners[:, None] == owners[None, :]) & (row_order[:, None] < row_order[None, :])
    return jnp.sum(same_owner.astype(jnp.int32), axis=0)


def tail(raw_logits, sumsq, width, owners, allowed, counts):
    vocab_count = lax.axis_size("vocab")
    vocab_index = lax.axis_index("vocab")
    own_rows, columns = raw_logits.shape
    blocks_here = columns // BLOCK
    list_width = allowed.shape[1]
    per_owner = 2 * own_rows // vocab_count
    positions = jnp.arange(list_width, dtype=jnp.int32)
    slot_rank = slot_ranks(owners)
    mine = jnp.where(positions[None, :] < counts[:, None], allowed, -1) - vocab_index * blocks_here
    here = jnp.arange(blocks_here, dtype=jnp.int32)
    present = jnp.any(mine[:, None, :] == here[None, :, None], axis=2).astype(jnp.int32)
    place = jnp.sum(jnp.where(here[:, None] < here[None, :], present[:, :, None], 0), axis=1)
    place = jnp.where(present > 0, place, -1)
    target_row = owners * per_owner + slot_rank
    slots = jnp.arange(vocab_count * per_owner, dtype=jnp.int32)
    to_slot = (target_row[None, :] == slots[:, None]).astype(jnp.float32)
    slot_index = jnp.arange(per_owner, dtype=jnp.int32)[:, None]
    owned_slot = ((owners[None, :] == vocab_index) & (slot_rank[None, :] == slot_index)).astype(
        jnp.int32
    )
    slot_lists = jnp.sum(owned_slot[:, :, None] * allowed[None, :, :], axis=1)
    slot_counts = jnp.sum(owned_slot * counts[None, :], axis=1)
    live_entry = positions[None, :] < slot_counts[:, None]
    source = jnp.clip(slot_lists // blocks_here, 0, vocab_count - 1)
    rank = jnp.zeros_like(source)
    for back in range(1, KMAX):
        earlier = jnp.pad(source, ((0, 0), (back, 0)), constant_values=-1)[:, :list_width]
        rank = rank + (earlier == source).astype(jnp.int32)
    table_row = (source * per_owner + slot_index) * (KMAX + 1) + jnp.minimum(rank, KMAX - 1)
    table_row = jnp.where(live_entry, table_row, 0)
    logits = raw_logits * lax.rsqrt(sumsq / width + EPSILON)[:, None]
    row_top = jnp.max(logits, axis=1)
    row_total = jnp.sum(jnp.exp(logits - row_top[:, None]), axis=1)
    picked = []
    for k in range(KMAX):
        chosen = jnp.zeros((own_rows, BLOCK), jnp.float32)
        for b in range(blocks_here):
            block = logits[:, b * BLOCK : (b + 1) * BLOCK]
            chosen = jnp.where((place[:, b] == k)[:, None], block, chosen)
        picked.append(chosen)
    lane = jnp.arange(BLOCK, dtype=jnp.int32)[None, :]
    picked.append(
        jnp.where(lane == 0, row_top[:, None], jnp.where(lane == 1, row_total[:, None], 0.0))
    )
    payload = jnp.concatenate(picked, axis=1)
    outgoing = jnp.dot(
        to_slot, payload, precision=lax.Precision.HIGHEST, preferred_element_type=jnp.float32
    ).reshape(vocab_count, per_owner, (KMAX + 1) * BLOCK)
    incoming = lax.all_to_all(outgoing, "vocab", split_axis=0, concat_axis=0, tiled=True)
    tops = incoming[:, :, KMAX * BLOCK]
    totals = incoming[:, :, KMAX * BLOCK + 1]
    big_top = jnp.max(tops, axis=0)
    big_total = jnp.sum(totals * jnp.exp(tops - big_top[None, :]), axis=0)
    shift = big_top + jnp.log(big_total)
    received = incoming.reshape(vocab_count * per_owner * (KMAX + 1), BLOCK)
    gathered = jnp.take(received, table_row, axis=0)
    return jnp.where(live_entry[:, :, None], gathered - shift[:, None, None], 0.0)


def body(partials, residual, norm_gain, head_weight, owners, allowed, counts):
    summed = lax.psum_scatter(partials, "tp", scatter_dimension=2, tiled=True)[0]
    hidden_rows = summed + residual.astype(jnp.float32)
    every_row = lax.all_gather(hidden_rows, "vocab", axis=0, tiled=True)
    square_part = jnp.sum(every_row * every_row, axis=1)
    scaled = (every_row * norm_gain).astype(jnp.bfloat16)
    head_terms = jnp.dot(scaled, head_weight, preferred_element_type=jnp.float32)
    raw_logits = lax.psum_scatter(head_terms, "tp", scatter_dimension=0, tiled=True)
    sumsq = lax.psum_scatter(square_part, "tp", scatter_dimension=0, tiled=True)
    width = head_weight.shape[0] * lax.axis_size("tp")
    return tail(raw_logits, sumsq, width, owners, allowed, counts)


def solution(mesh):
    placed = (
        P("tp", "vocab", None),
        P("vocab", "tp"),
        P("tp"),
        P("tp", "vocab"),
        P("tp"),
        P("tp", None),
        P("tp"),
    )
    return jax.shard_map(
        body, mesh=mesh, in_specs=placed, out_specs=P(("tp", "vocab"), None, None), check_vma=False
    )
```

profile of v0, /device:TPU:1, one launch (start us, length us, event | category | flops | bytes accessed | tf_op | source)
XLA Modules:
  0.0 280.3 jit_solution(17336991937507651582)
XLA Ops:
  6.5 0.0 copy-start
  6.5 0.0 reduce-scatter.3.cloned.1.call-start
  6.5 0.7 reduce-scatter.3.cloned.1.call-update
  7.3 0.0 all-gather.2.cloned.1.call-start
  7.3 43.3 %reduce-scatter.3.cloned.1.call-done = f32[1,16,1024]{2,1,0:T(8,128)} async-done(((f32[1,16,8192]{2,1,0:T(8,128)}), f32[1,16,1024]{2,1,0:T(8,128)}) %reduce-scatter.3.cloned.1.call-update) | async-done | bytes 65552 | tf_op jit(solution)/shard_map/reduce_scatter | solution.py:78
  50.6 1.5 bitcast_add_fusion
  52.1 0.0 all-gather.2.cloned.1.call-update
  52.1 0.0 reduce-scatter.5.cloned.1.call-start
  52.2 91.4 %all-gather.2.cloned.1.call-done = f32[1024,1024]{1,0:T(8,128)} async-done(((f32[16,1024]{1,0:T(8,128)}), f32[1024,1024]{1,0:T(8,128)}) %all-gather.2.cloned.1.call-update) | async-done | bytes 4194320 | tf_op jit(solution)/shard_map/all_gather | solution.py:80
  143.6 0.0 copy-done
  143.6 7.5 %fusion = f32[1024,1536]{1,0:T(8,128)} fusion(bf16[1024,1536]{1,0:T(8,128)(2,1)S(1)} %copy-done, f32[1024,1024]{1,0:T(8,128)} %all-gather.2.cloned.1.call-done, f32[1024]{0:T(1024)} %param.9), kind=kOutput, calls=%fused_computation.3 | convolution fusion | flops 3223322624 | bytes 13635584 | tf_op jit(solution)/shard_map/dot_general | solution.py:83
  151.2 0.0 copy-start.1
  151.2 0.0 copy-start.2
  151.2 0.0 copy-start.3
  151.2 0.0 reduce-scatter.5.cloned.1.call-update
  151.2 0.9 copy-done.1
  152.1 0.0 copy-done.2
  152.1 0.1 select_subtract_fusion
  152.2 0.3 fusion.2
  152.5 1.3 dynamic-slice
  154.4 0.0 copy-done.3
  154.4 0.1 convert_reduce_fusion
  154.5 0.1 select_reduce_fusion
  154.7 2.5 multiply_reduce_fusion
  157.3 14.9 %all-reduce.3 = f32[1024]{0:T(1024)S(1)} all-reduce(f32[1024]{0:T(1024)S(1)} %multiply_reduce_fusion), channel_id=4, replica_groups=mesh['tp'=8,'vocab'=64] {'tp'}, use_global_device_ids=true, to_apply=%region_8.9.clone | all-reduce | flops 1024 | bytes 8192
  172.1 0.1 fusion.17
  172.2 53.1 %reduce-scatter.5.cloned.1.call-done = f32[128,1536]{1,0:T(8,128)} async-done(((f32[1024,1536]{1,0:T(8,128)}), f32[128,1536]{1,0:T(8,128)}) %reduce-scatter.5.cloned.1.call-update) | async-done | bytes 786448 | tf_op jit(solution)/shard_map/reduce_scatter | solution.py:84
  225.3 1.3 fusion.18
  226.6 0.3 exponential_reduce_fusion
  226.9 0.3 select_dynamic-update-slice_fusion.4
  227.2 0.3 select_dynamic-update-slice_fusion.3
  227.4 0.3 select_dynamic-update-slice_fusion.2
  227.7 0.3 select_dynamic-update-slice_fusion.1
  228.0 0.1 select_dynamic-update-slice_fusion
  228.1 1.3 fusion.3
  229.4 2.1 reshape.93
  231.5 11.1 %all-to-all-start = ((f32[64,4,640]{2,1,0:T(4,128)}), f32[64,4,640]{2,1,0:T(4,128)}, u32[]{:S(2)}, u32[]{:S(2)}) async-start(f32[64,4,640]{2,1,0:T(4,128)} %reshape.93), calls=%async_computation.2 | async-start | bytes 1310720 | tf_op jit(solution)/shard_map/all_to_all | solution.py:66
  242.6 0.1 select_reduce_fusion.1
  242.8 0.2 multiply_reduce_fusion.1
  242.9 0.1 compare_and_fusion
  243.0 19.6 %all-to-all-done = f32[64,4,640]{2,1,0:T(4,128)} async-done(((f32[64,4,640]{2,1,0:T(4,128)}), f32[64,4,640]{2,1,0:T(4,128)}, u32[]{:S(2)}, u32[]{:S(2)}) %all-to-all-start) | async-done | bytes 655392 | tf_op jit(solution)/shard_map/all_to_all | solution.py:66
  262.7 1.2 fusion.19
  263.9 0.1 copy.17
  264.0 0.1 copy.18
  264.1 0.2 fusion.13
  264.3 2.2 reshape.94
  266.5 5.1 %gather_fusion = f32[1024,128]{1,0:T(8,128)} fusion(f32[1280,128]{1,0:T(8,128)} %reshape.94, s32[1024]{0:T(1024)S(1)} %broadcast_clamp_fusion), kind=kCustom, calls=%fused_computation | custom fusion | bytes 1052672 | tf_op jit(solution)/shard_map/jit(_take)/gather | solution.py:73
  271.6 2.2 subtract_select_fusion
  (14 shorter events, 0.1 us)
Async XLA Ops:
  6.5 137.1 %copy-start = (bf16[1024,1536]{1,0:T(8,128)(2,1)S(1)}, bf16[1024,1536]{1,0:T(8,128)(2,1)}, u32[]{:S(2)}) copy-start(bf16[1024,1536]{1,0:T(8,128)(2,1)} %param.10) | copy-start | bytes 9437188
  6.5 44.1 %reduce-scatter.3.cloned.1.call-start = ((), (), s32[]{:S(2)}) async-start(), calls=%async_computation.3 | async-start | bytes 589824 | tf_op jit(solution)/shard_map/reduce_scatter | solution.py:78
  7.3 136.4 %all-gather.2.cloned.1.call-start = ((), (), s32[]{:S(2)}) async-start(), calls=%async_computation.4 | async-start | bytes 4259840 | tf_op jit(solution)/shard_map/all_gather | solution.py:80
  52.1 173.1 %reduce-scatter.5.cloned.1.call-start = ((), (), s32[]{:S(2)}) async-start(), calls=%async_computation.5 | async-start | bytes 7077888 | tf_op jit(solution)/shard_map/reduce_scatter | solution.py:84
  151.2 0.9 copy-start.1
  151.2 0.9 copy-start.2
  151.2 3.2 %copy-start.3 = (s32[128]{0:T(128)S(1)}, s32[128]{0:T(128)}, u32[]{:S(2)}) copy-start(s32[128]{0:T(128)} %param.11) | copy-start | bytes 1540
  231.5 31.2 %all-to-all-start = ((f32[64,4,640]{2,1,0:T(4,128)}), f32[64,4,640]{2,1,0:T(4,128)}, u32[]{:S(2)}, u32[]{:S(2)}) async-start(f32[64,4,640]{2,1,0:T(4,128)} %reshape.93), calls=%async_computation.2 | async-start | bytes 1310720 | tf_op jit(solution)/shard_map/all_to_all | solution.py:66
Sparse Core Ops, SparseCore 0:
  10.1 40.4 reduce-scatter.2
  54.0 89.5 all-gather.1
  151.3 73.9 reduce-scatter.4
where the time goes:
time: 281 us; the launch traced here: 280 us
  waiting for transfers between devices  208 us (74%)
  blocking collectives  14.9 us (5%)
  between operations  14 us (5%)
  local copies, waits for them, and re-layouts  11.8 us (4%)
  other arithmetic  11.5 us (4%)
  starting transfers between devices  11.2 us (4%)
  matrix products  8.81 us (3%)
    all_gather x1, waiting for transfers between devices, body(): every_row = lax.all_gather(hidden_rows, 'vocab', axis=0, tiled=True)  91.4 us
    reduce_scatter x1, waiting for transfers between devices, body(): lax.psum_scatter(head_terms, 'tp', scatter_dimension=0, tiled=True)  53.1 us
    reduce_scatter x1, waiting for transfers between devices, body(): lax.psum_scatter(partials, 'tp', scatter_dimension=2, tiled=True)[0]  43.3 us
    all_to_all x1, waiting for transfers between devices, tail(): lax.all_to_all(outgoing, 'vocab', split_axis=0, concat_axis=0, tiled=True)  19.6 us
    unnamed x1, blocking collectives  14.9 us
    all_to_all x1, starting transfers between devices, tail(): lax.all_to_all(outgoing, 'vocab', split_axis=0, concat_axis=0, tiled=True)  11.1 us
    dot_general x1, matrix products, body(): jnp.dot(scaled, head_weight, preferred_element_type=jnp.float32)  7.54 us
  transfers between devices with their start and end apart: 4, of which 4 were waited for; matrix products, arithmetic and copies ran while one was open for 2% of the time, Pallas kernels for 0%

commit v1 on v0

--- a/solution.py
+++ b/solution.py
@@ -6,6 +6,12 @@
 EPSILON = 1e-05
 BLOCK = 128
 KMAX = 4
+
+
+def divide_target(m):
+    val2 = jnp.stack([m for _ in range(lax.axis_size("vocab"))])
+    aux = lax.all_to_all(val2, "vocab", 0, 0)
+    return jnp.concatenate(aux, 0)
 
 
 def slot_ranks(owners):
@@ -77,7 +83,7 @@
 def body(partials, residual, norm_gain, head_weight, owners, allowed, counts):
     summed = lax.psum_scatter(partials, "tp", scatter_dimension=2, tiled=True)[0]
     hidden_rows = summed + residual.astype(jnp.float32)
-    every_row = lax.all_gather(hidden_rows, "vocab", axis=0, tiled=True)
+    every_row = divide_target(hidden_rows)
     square_part = jnp.sum(every_row * every_row, axis=1)
     scaled = (every_row * norm_gain).astype(jnp.bfloat16)
     head_terms = jnp.dot(scaled, head_weight, preferred_element_type=jnp.float32)

time: 281 us -> 299 us (1.064)
  blocking collectives: 14.9 us -> 126 us
  waiting for transfers between devices: 208 us -> 115 us
    all_to_all x0 -> x1, blocking collectives: none -> 112 us  [divide_target(): aux = lax.all_to_all(val2, 'vocab', 0, 0)]
    all_gather x1 -> x0, waiting for transfers between devices: 91.4 us -> none  [body(): every_row = lax.all_gather(hidden_rows, 'vocab', axis=0, tiled=True)]
  transfers between devices with their start and end apart: 4 -> 3, of which waited for: 4 -> 3; matrix products, arithmetic and copies ran while one was open for 2% -> 2% of each run, Pallas kernels for 0% -> 0%
where the time goes in v1:
time: 299 us; the launch traced here: 298 us
  blocking collectives  126 us (42%)
  waiting for transfers between devices  115 us (38%)
  between operations  14.3 us (5%)
  local copies, waits for them, and re-layouts  13.8 us (5%)
  other arithmetic  11.5 us (4%)
  starting transfers between devices  11.1 us (4%)
  matrix products  6.58 us (2%)
    all_to_all x1, blocking collectives, divide_target(): aux = lax.all_to_all(val2, 'vocab', 0, 0)  112 us
    reduce_scatter x1, waiting for transfers between devices, body(): lax.psum_scatter(head_terms, 'tp', scatter_dimension=0, tiled=True)  51.8 us
    reduce_scatter x1, waiting for transfers between devices, body(): lax.psum_scatter(partials, 'tp', scatter_dimension=2, tiled=True)[0]  43.3 us
    all_to_all x1, waiting for transfers between devices, tail(): lax.all_to_all(outgoing, 'vocab', split_axis=0, concat_axis=0, tiled=True)  19.6 us
    unnamed x1, blocking collectives  13.6 us
    all_to_all x1, starting transfers between devices, tail(): lax.all_to_all(outgoing, 'vocab', split_axis=0, concat_axis=0, tiled=True)  11.1 us
  transfers between devices with their start and end apart: 3, of which 3 were waited for; matrix products, arithmetic and copies ran while one was open for 2% of the time, Pallas kernels for 0%

profile of v1, /device:TPU:1, one launch (start us, length us, event | category | flops | bytes accessed | tf_op | source)
XLA Modules:
  0.0 298.4 jit_solution(8261845734032989033)
XLA Ops:
  6.5 0.0 copy-start
  6.5 0.0 reduce-scatter.3.cloned.1.call-start
  6.5 0.7 reduce-scatter.3.cloned.1.call-update
  7.3 0.0 reduce-scatter.5.cloned.1.call-start
  7.3 43.3 %reduce-scatter.3.cloned.1.call-done = f32[1,16,1024]{2,1,0:T(8,128)} async-done(((f32[1,16,8192]{2,1,0:T(8,128)}), f32[1,16,1024]{2,1,0:T(8,128)}) %reduce-scatter.3.cloned.1.call-update) | async-done | bytes 65552 | tf_op jit(solution)/shard_map/reduce_scatter | solution.py:84
  50.6 0.8 bitcast_add_fusion
  51.5 0.5 stack.2
  52.0 0.0 copy-start.3
  52.0 112.0 %all_to_all.10 = f32[64,16,1024]{2,1,0:T(8,128)S(1)} all-to-all(f32[64,16,1024]{2,1,0:T(8,128)S(1)} %stack.2), channel_id=1, replica_groups=mesh['tp'=8,'vocab'=64] {'vocab'}, dimensions={0} | all-to-all | bytes 8388608 | tf_op jit(solution)/shard_map/all_to_all | solution.py:13
  164.0 0.0 copy-done.3
  164.0 0.0 copy-start.1
  164.0 0.6 fusion
  164.6 1.4 copy-done.1
  166.1 0.0 copy-done
  166.1 5.3 %fusion.19 = f32[1024,1536]{1,0:T(8,128)} fusion(bf16[1024,1024]{1,0:T(8,128)(2,1)S(1)} %fusion, bf16[1024,1536]{1,0:T(8,128)(2,1)S(1)} %copy-done), kind=kOutput, calls=%fused_computation.109 | convolution fusion | flops 3221225472 | bytes 11534336 | tf_op jit(solution)/shard_map/dot_general | solution.py:89
  171.4 0.0 copy-start.2
  171.4 0.0 copy-start.4
  171.4 0.0 copy-start.5
  171.4 0.0 reduce-scatter.5.cloned.1.call-update
  171.4 0.9 copy-done.2
  172.3 0.0 copy-done.4
  172.3 0.1 select_subtract_fusion
  172.4 0.3 fusion.1
  172.7 1.3 dynamic-slice
  174.6 0.0 copy-done.5
  174.7 0.1 convert_reduce_fusion
  174.8 0.1 select_reduce_fusion
  175.0 2.5 multiply_reduce_fusion
  177.5 0.1 reduce_sum.70
  177.6 13.6 %all-reduce.3 = f32[1024]{0:T(1024)S(1)} all-reduce(f32[1024]{0:T(1024)S(1)} %reduce_sum.70), channel_id=4, replica_groups=mesh['tp'=8,'vocab'=64] {'tp'}, use_global_device_ids=true, to_apply=%region_8.9.clone | all-reduce | flops 1024 | bytes 8192
  191.2 0.1 fusion.16
  191.3 51.8 %reduce-scatter.5.cloned.1.call-done = f32[128,1536]{1,0:T(8,128)} async-done(((f32[1024,1536]{1,0:T(8,128)}), f32[128,1536]{1,0:T(8,128)}) %reduce-scatter.5.cloned.1.call-update) | async-done | bytes 786448 | tf_op jit(solution)/shard_map/reduce_scatter | solution.py:90
  243.1 1.3 fusion.17
  244.4 0.3 exponential_reduce_fusion
  244.7 0.3 select_dynamic-update-slice_fusion.4
  245.0 0.3 select_dynamic-update-slice_fusion.3
  245.2 0.3 select_dynamic-update-slice_fusion.2
  245.5 0.3 select_dynamic-update-slice_fusion.1
  245.8 0.1 select_dynamic-update-slice_fusion
  245.9 1.3 fusion.2
  247.2 2.1 reshape.100
  249.3 11.1 %all-to-all-start.1 = ((f32[64,4,640]{2,1,0:T(4,128)}), f32[64,4,640]{2,1,0:T(4,128)}, u32[]{:S(2)}, u32[]{:S(2)}) async-start(f32[64,4,640]{2,1,0:T(4,128)} %reshape.100), calls=%async_computation.3 | async-start | bytes 1310720 | tf_op jit(solution)/shard_map/all_to_all | solution.py:72
  260.4 0.1 select_reduce_fusion.1
  260.5 0.2 multiply_reduce_fusion.1
  260.7 0.1 compare_and_fusion
  260.8 19.6 %all-to-all-done.1 = f32[64,4,640]{2,1,0:T(4,128)} async-done(((f32[64,4,640]{2,1,0:T(4,128)}), f32[64,4,640]{2,1,0:T(4,128)}, u32[]{:S(2)}, u32[]{:S(2)}) %all-to-all-start.1) | async-done | bytes 655392 | tf_op jit(solution)/shard_map/all_to_all | solution.py:72
  280.4 1.2 fusion.18
  281.7 0.1 copy.17
  281.8 0.1 copy.18
  281.9 0.2 fusion.12
  282.1 2.2 reshape.101
  284.3 5.1 %gather_fusion = f32[1024,128]{1,0:T(8,128)} fusion(f32[1280,128]{1,0:T(8,128)} %reshape.101, s32[1024]{0:T(1024)S(1)} %broadcast_clamp_fusion), kind=kCustom, calls=%fused_computation | custom fusion | bytes 1052672 | tf_op jit(solution)/shard_map/jit(_take)/gather | solution.py:79
  289.4 2.2 subtract_select_fusion
  (14 shorter events, 0.1 us)
Async XLA Ops:
  6.5 159.5 %copy-start = (bf16[1024,1536]{1,0:T(8,128)(2,1)S(1)}, bf16[1024,1536]{1,0:T(8,128)(2,1)}, u32[]{:S(2)}) copy-start(bf16[1024,1536]{1,0:T(8,128)(2,1)} %param.10) | copy-start | bytes 9437188
  6.5 44.1 %reduce-scatter.3.cloned.1.call-start = ((), (), s32[]{:S(2)}) async-start(), calls=%async_computation.4 | async-start | bytes 589824 | tf_op jit(solution)/shard_map/reduce_scatter | solution.py:84
  7.3 235.8 %reduce-scatter.5.cloned.1.call-start = ((), (), s32[]{:S(2)}) async-start(), calls=%async_computation.5 | async-start | bytes 7077888 | tf_op jit(solution)/shard_map/reduce_scatter | solution.py:90
  52.0 112.0 %copy-start.3 = (f32[1024]{0:T(1024)S(1)}, f32[1024]{0:T(1024)}, u32[]{:S(2)}) copy-start(f32[1024]{0:T(1024)} %param.9) | copy-start | bytes 12292
  164.0 2.0 copy-start.1
  171.4 0.9 copy-start.2
  171.4 0.9 copy-start.4
  171.4 3.2 %copy-start.5 = (s32[128]{0:T(128)S(1)}, s32[128]{0:T(128)}, u32[]{:S(2)}) copy-start(s32[128]{0:T(128)} %param.11) | copy-start | bytes 1540
  249.3 31.1 %all-to-all-start.1 = ((f32[64,4,640]{2,1,0:T(4,128)}), f32[64,4,640]{2,1,0:T(4,128)}, u32[]{:S(2)}, u32[]{:S(2)}) async-start(f32[64,4,640]{2,1,0:T(4,128)} %reshape.100), calls=%async_computation.3 | async-start | bytes 1310720 | tf_op jit(solution)/shard_map/all_to_all | solution.py:72
Sparse Core Ops, SparseCore 0:
  10.1 40.4 reduce-scatter.2
  171.5 71.4 reduce-scatter.4
